TPU v7x, 32 devices: a whole 2x2x4 slice. The times are simulated.
32 devices in a mesh: fsdp: 4 (over y, x), ctx: 4 (over z), tp: 2 (over core).
Axes of the slice: x: 2, y: 2, z: 4, core: 2. Of those that a mesh axis runs over, the one named last changes fastest.
Arguments:
- tokens: bfloat16 [2, 2, 4, 128, 2304], P(None, None, 'ctx', 'fsdp'), may hold values from -6 to 6
- segments: int32 [2, 2, 4, 128], P(None, None, 'ctx', 'fsdp'), may hold values from 0 to 3, as said below
- stretch_order: int32 [4], replicated, may hold values from 0 to 3, as said below
- norm_gains: float32 [4, 2304], replicated, may hold values from 0.25 to 1.75
- query_proj: bfloat16 [2304, 2048], P('fsdp', 'tp'), may hold values from -0.125 to 0.125
- keyval_proj: bfloat16 [2304, 2, 1024], P('fsdp', None, 'tp'), may hold values from -0.125 to 0.125
- attn_proj: bfloat16 [2304, 2048], P('fsdp', 'tp'), may hold values from -0.125 to 0.125
- ffn_in: bfloat16 [2304, 2, 9216], P('fsdp', None, 'tp'), may hold values from -0.125 to 0.125
- ffn_out: bfloat16 [2304, 9216], P('fsdp', 'tp'), may hold values from -0.0625 to 0.0625
- cotangent: bfloat16 [2, 2, 4, 128, 2304], P(None, None, 'ctx', 'fsdp'), may hold values from -6 to 6
Outputs:
- result: bfloat16 [2, 2, 4, 128, 2304], P(None, None, 'ctx', 'fsdp')
- grad_tokens: float32 [2, 2, 4, 128, 2304], P(None, None, 'ctx', 'fsdp')
- grad_gains: float32 [4, 2304], replicated
- grad_query: float32 [2304, 2048], P('fsdp', 'tp')
- grad_keyval: float32 [2304, 2, 1024], P('fsdp', None, 'tp')
- grad_attn: float32 [2304, 2048], P('fsdp', 'tp')
- grad_ffn_in: float32 [2304, 2, 9216], P('fsdp', None, 'tp')
- grad_ffn_out: float32 [2304, 9216], P('fsdp', 'tp')
Inputs may be any that keep to these rules, and one draw needn't show every extreme that they name: `segments`: along the positions of a sequence the segment ids never fall; every sequence holds exactly four documents, ids 0 to 3. Each of 0 to 3 once; slot c holds position blocks stretch_order[c] and 7 - stretch_order[c] of every sequence.
All inputs are finite; a program needn't handle non-finite values.
Results may differ from a plain program's by a relative error of at most 0.015.
Values may be sent and summed in bfloat16 or wider, within the bound.
No kernel may reach another device: no remote copies, remote signals or barrier semaphores. Data moves between devices by JAX's collectives and lax.ppermute only.
A program may use at most 640 MiB of HBM per device.

v0:
```python
import jax
import jax.numpy as jnp
from jax import lax
from jax.sharding import PartitionSpec as P

HEAD_DIM = 256
SOFT_CAP = 50.0
NORM_EPS = 1e-06
F32 = jnp.float32
BF16 = jnp.bfloat16


def rms_factor(values):
    return lax.rsqrt(jnp.mean(values * values, axis=-1, keepdims=True) + NORM_EPS)


def norm_back(grad_out, values, scale_gain):
    factor = rms_factor(values)
    normed = values * factor
    grad_gain = jnp.sum(grad_out * normed, axis=0)
    scaled_grad = grad_out * scale_gain
    grad_in = factor * (
        scaled_grad - normed * jnp.mean(scaled_grad * normed, axis=-1, keepdims=True)
    )
    return (grad_in, grad_gain)


def gelu_parts(gate_vals):
    values, pullback = jax.vjp(lambda inputs: jax.nn.gelu(inputs, approximate=True), gate_vals)
    return (values, pullback(jnp.ones_like(gate_vals))[0])


def dot_nn(left, right):
    return jnp.dot(left, right, preferred_element_type=F32)


def dot_nt(left, right):
    return lax.dot_general(left, right, (((1,), (1,)), ((), ())), preferred_element_type=F32)


def dot_tn(left, right):
    return lax.dot_general(left, right, (((0,), (0,)), ((), ())), preferred_element_type=F32)


def swap(values, axis_name, offset):
    count = lax.axis_size(axis_name)
    return lax.ppermute(values, axis_name, [(i, i ^ offset) for i in range(count)])


def gather_xor(values, axis_name):
    count = lax.axis_size(axis_name)
    return jnp.stack([values] + [swap(values, axis_name, j) for j in range(1, count)])


def scatter_xor(parts, axis_name):
    total = parts[0].astype(F32)
    for j in range(1, lax.axis_size(axis_name)):
        total = total + swap(parts[j].astype(BF16), axis_name, j).astype(F32)
    return total


def gather_rows(rows):
    near = gather_xor(rows, "ctx").reshape(-1, rows.shape[-1])
    return gather_xor(near, "tp").reshape(-1, rows.shape[-1])


def scatter_rows(partial):
    width = partial.shape[-1]
    near = scatter_xor(partial.reshape(lax.axis_size("tp"), -1, width), "tp")
    return scatter_xor(near.reshape(lax.axis_size("ctx"), -1, width), "ctx")


def sum_all(values):
    for axis_name in ("tp", "ctx", "fsdp"):
        offset = 1
        while offset < lax.axis_size(axis_name):
            values = values + swap(values, axis_name, offset)
            offset *= 2
    return values


def xor_order(values, own_at, axis):
    offset = 1
    while offset < values.shape[axis]:
        halves = values.reshape(values.shape[:axis] + (-1, 2, offset) + values.shape[axis + 1 :])
        turned = jnp.flip(halves, axis + 1)
        if isinstance(own_at, int):
            picked = turned if own_at & offset else halves
        else:
            picked = jnp.where(own_at & offset != 0, turned, halves)
        values = picked.reshape(values.shape)
        offset *= 2
    return values


def cols(values, start, width):
    return lax.dynamic_slice_in_dim(values, start, width, axis=values.ndim - 1)


def on_device(
    tokens,
    segments,
    stretch_order,
    norm_gains,
    query_proj,
    keyval_proj,
    attn_proj,
    ffn_in,
    ffn_out,
    cotangent,
):
    seq_count, _, _, half_dev, width = tokens.shape
    fsdp_count = lax.axis_size("fsdp")
    ctx_count = lax.axis_size("ctx")
    tp_count = lax.axis_size("tp")
    fsdp_at, ctx_at, tp_at = (lax.axis_index(name) for name in ("fsdp", "ctx", "tp"))
    row_count = seq_count * 2 * half_dev
    own_count = row_count // tp_count
    group_rows = own_count * tp_count * ctx_count
    assert seq_count == tp_count
    head_count = query_proj.shape[1] // HEAD_DIM
    group = head_count // (keyval_proj.shape[2] // HEAD_DIM)
    repeat = ctx_count // head_count
    assert repeat >= 1 and repeat * head_count == ctx_count
    sharers = group * repeat
    head_at = ctx_at // repeat
    kv_at = ctx_at // sharers
    share_at = ctx_at % sharers
    q_width = HEAD_DIM // repeat
    kv_width = 2 * HEAD_DIM // sharers
    q_own = ctx_at % repeat * q_width
    kv_own = share_at * kv_width
    ff_width = ffn_out.shape[1] // ctx_count
    ff_at = ctx_at * ff_width
    qkv_part = jnp.concatenate(
        [
            cols(query_proj, head_at * HEAD_DIM, HEAD_DIM),
            cols(keyval_proj[:, 0], kv_at * HEAD_DIM, HEAD_DIM),
            cols(keyval_proj[:, 1], kv_at * HEAD_DIM, HEAD_DIM),
        ],
        axis=1,
    )
    attn_part = cols(attn_proj, head_at * HEAD_DIM, HEAD_DIM)
    in_part = jnp.concatenate(
        [cols(ffn_in[:, 0], ff_at, ff_width), cols(ffn_in[:, 1], ff_at, ff_width)], axis=1
    )
    out_part = cols(ffn_out, ff_at, ff_width)
    w_qkv, w_attn, w_in, w_out = (
        lax.all_gather(part, "fsdp", axis=0, tiled=True)
        for part in (qkv_part, attn_part, in_part, out_part)
    )
    gain_pre, gain_post, gain_ffn, gain_last = (norm_gains[i] for i in range(4))
    row_at = tp_at * own_count
    tok_in = lax.dynamic_slice_in_dim(
        tokens.reshape(row_count, width), row_at, own_count, 0
    ).astype(F32)
    cot_in = lax.dynamic_slice_in_dim(
        cotangent.reshape(row_count, width), row_at, own_count, 0
    ).astype(F32)
    half_stretch = half_dev * fsdp_count
    seg_all = lax.all_gather(
        segments.reshape(seq_count, 2, half_dev), ("fsdp", "ctx"), axis=0, tiled=False
    ).reshape(fsdp_count, ctx_count, seq_count, 2, half_dev)
    ctx_ids = ctx_at ^ jnp.arange(ctx_count)
    fsdp_ids = fsdp_at ^ jnp.arange(fsdp_count)
    key_seg = xor_order(xor_order(xor_order(seg_all, fsdp_at, 0), ctx_at, 1), tp_at, 2)
    key_seg = key_seg.transpose(2, 0, 1, 3, 4)
    query_seg = key_seg[:, 0].reshape(seq_count, -1)
    key_seg = key_seg.reshape(seq_count, -1)
    paired = xor_order(stretch_order, ctx_at, 0)
    blocks = jnp.stack([paired, 2 * ctx_count - 1 - paired], axis=1)
    key_pos = (
        blocks[None, :, :, None] * half_stretch
        + fsdp_ids[:, None, None, None] * half_dev
        + jnp.arange(half_dev)[None, None, None, :]
    )
    query_pos = key_pos[0].reshape(-1)
    key_pos = key_pos.reshape(-1)
    allowed = (query_seg[:, :, None] == key_seg[:, None, :]) & (
        key_pos[None, None, :] <= query_pos[None, :, None]
    )
    xnorm_own = (tok_in * rms_factor(tok_in) * gain_pre).astype(BF16)
    xnorm = gather_rows(xnorm_own)
    qkv = dot_nn(xnorm, w_qkv).astype(BF16)
    query = qkv[:, :HEAD_DIM].reshape(seq_count, -1, HEAD_DIM)
    kv_own_rows = qkv[:, HEAD_DIM:].reshape(seq_count, -1, 2 * HEAD_DIM)
    kv_all = jnp.concatenate(
        [kv_own_rows] + [swap(kv_own_rows, "fsdp", j) for j in range(1, fsdp_count)], axis=1
    )
    keys, vals = (kv_all[:, :, :HEAD_DIM], kv_all[:, :, HEAD_DIM:])
    raw_scores = jnp.einsum("sqe,ske->sqk", query, keys, preferred_element_type=F32)
    capped = SOFT_CAP * jnp.tanh(raw_scores * (HEAD_DIM ** (-0.5) / SOFT_CAP))
    expo = jnp.where(allowed, jnp.exp(capped), 0.0)
    denom = jnp.sum(expo, axis=-1, keepdims=True)
    mixture = jnp.einsum("sqk,ske->sqe", expo.astype(BF16), vals, preferred_element_type=F32)
    attended_seq = (mixture / denom).astype(BF16)
    lse = jnp.log(denom)
    attended = attended_seq.reshape(group_rows, HEAD_DIM)
    attended_own = attended if repeat == 1 else cols(attended, q_own, q_width)
    w_attn_own = w_attn if repeat == 1 else cols(w_attn, q_own, q_width)
    branch = scatter_rows(dot_nt(attended_own, w_attn_own))
    hidden = tok_in + branch * rms_factor(branch) * gain_post
    hnorm = gather_rows((hidden * rms_factor(hidden) * gain_ffn).astype(BF16))
    both = dot_nn(hnorm, w_in)
    gate, up = (both[:, :ff_width], both[:, ff_width:])
    gelu_vals, gelu_slope = gelu_parts(gate)
    middle = (gelu_vals * up).astype(BF16)
    ffout = scatter_rows(dot_nt(middle, w_out))
    result = (hidden + ffout * rms_factor(ffout) * gain_last).astype(BF16)
    grad_ff, grad_last_gain = norm_back(cot_in, ffout, gain_last)
    grad_ffb = gather_rows(grad_ff.astype(BF16))
    grad_mid = dot_nn(grad_ffb, w_out)
    grad_both = jnp.concatenate([grad_mid * up * gelu_slope, grad_mid * gelu_vals], axis=1).astype(
        BF16
    )

    def weight_grad(left, right):
        return lax.psum_scatter(
            dot_tn(left, right).astype(BF16), "fsdp", scatter_dimension=0, tiled=True
        )

    def spread(part):
        return lax.all_gather(part, "ctx", axis=0, tiled=False)

    all_out = spread(weight_grad(grad_ffb, middle))
    all_in = spread(weight_grad(hnorm, grad_both))
    grad_hn = scatter_rows(dot_nt(grad_both, w_in))
    grad_hid_n, grad_ffn_gain = norm_back(grad_hn, hidden, gain_ffn)
    grad_hidden = cot_in + grad_hid_n
    grad_branch, grad_post_gain = norm_back(grad_hidden, branch, gain_post)
    grad_branchb = gather_rows(grad_branch.astype(BF16))
    grad_attended = dot_nn(grad_branchb, w_attn).astype(BF16)
    grad_att_seq = grad_attended.reshape(seq_count, -1, HEAD_DIM)
    delta = jnp.sum(grad_att_seq.astype(F32) * attended_seq.astype(F32), axis=-1, keepdims=True)
    prob = jnp.where(allowed, jnp.exp(capped - lse), 0.0)
    grad_prob = jnp.einsum("sqe,ske->sqk", grad_att_seq, vals, preferred_element_type=F32)
    ratio = capped / SOFT_CAP
    grad_raw = prob * (grad_prob - delta) * (1.0 - ratio * ratio) * HEAD_DIM ** (-0.5)
    raw_half = grad_raw.astype(BF16)
    prob_half = prob.astype(BF16)
    grad_q = jnp.einsum("sqk,ske->sqe", raw_half, keys, preferred_element_type=F32).astype(BF16)
    grad_k = jnp.einsum("sqk,sqe->ske", raw_half, query, preferred_element_type=F32)
    grad_v = jnp.einsum("sqk,sqe->ske", prob_half, grad_att_seq, preferred_element_type=F32)
    pieces = jnp.stack([grad_k, grad_v])
    pieces = pieces.reshape(2, *grad_k.shape[:2], sharers // 2, kv_width)
    pieces = pieces.transpose(0, 3, 1, 2, 4).reshape(sharers, *grad_k.shape[:2], kv_width)
    kv_term = lax.dynamic_index_in_dim(pieces, share_at, 0, keepdims=False)
    for j in range(repeat, sharers, repeat):
        sent = lax.dynamic_index_in_dim(pieces, share_at ^ j, 0, keepdims=False).astype(BF16)
        by_ctx = sent.reshape(seq_count, fsdp_count, ctx_count, -1, kv_width)
        sent = xor_order(by_ctx, j, 2).reshape(sent.shape)
        kv_term = kv_term + swap(sent, "ctx", j).astype(F32)
    kv_term = kv_term.reshape(seq_count, fsdp_count, -1, kv_width).transpose(1, 0, 2, 3)
    grad_kv = scatter_xor(kv_term, "fsdp").astype(BF16).reshape(group_rows, kv_width)
    grad_q = grad_q.reshape(group_rows, HEAD_DIM)
    grad_q_own = grad_q if repeat == 1 else cols(grad_q, q_own, q_width)
    grad_qkv = jnp.concatenate([grad_q_own, grad_kv], axis=1)
    w_q_own = w_qkv[:, :HEAD_DIM] if repeat == 1 else cols(w_qkv, q_own, q_width)
    w_qkv_own = jnp.concatenate([w_q_own, cols(w_qkv, HEAD_DIM + kv_own, kv_width)], axis=1)
    grad_xnorm = scatter_rows(dot_nt(grad_qkv, w_qkv_own))
    grad_x_n, grad_pre_gain = norm_back(grad_xnorm, tok_in, gain_pre)
    grad_tokens_own = grad_hidden + grad_x_n
    all_attn = spread(weight_grad(grad_branchb, attended_own))
    all_qkv = spread(weight_grad(xnorm, grad_qkv))
    own_width = all_out.shape[1]
    grad_gains = sum_all(
        jnp.stack([grad_pre_gain, grad_post_gain, grad_ffn_gain, grad_last_gain], axis=0)
    )
    result = lax.all_gather(result, "tp", axis=0, tiled=True)
    grad_tokens = lax.all_gather(grad_tokens_own, "tp", axis=0, tiled=True)

    def columns(spread_grad):
        return jnp.moveaxis(spread_grad, 0, -2).astype(F32)

    grad_query = columns(all_qkv[:, :, :q_width]).reshape(own_width, -1)
    grad_keyval = (
        all_qkv[:, :, q_width:]
        .reshape(ctx_count // sharers, 2, sharers // 2, own_width, kv_width)
        .transpose(3, 1, 0, 2, 4)
        .astype(F32)
        .reshape(own_width, 2, -1)
    )
    grad_attn = columns(all_attn).reshape(own_width, -1)
    grad_ffn_in = columns(all_in.reshape(ctx_count, own_width, 2, ff_width)).reshape(
        own_width, 2, -1
    )
    grad_ffn_out = columns(all_out).reshape(own_width, -1)
    return (
        result.reshape(tokens.shape),
        grad_tokens.reshape(tokens.shape),
        grad_gains,
        grad_query,
        grad_keyval,
        grad_attn,
        grad_ffn_in,
        grad_ffn_out,
    )


def solution(mesh):
    placed = (
        P(None, None, "ctx", "fsdp", None),
        P(None, None, "ctx", "fsdp"),
        P(),
        P(),
        P("fsdp", "tp"),
        P("fsdp", None, "tp"),
        P("fsdp", "tp"),
        P("fsdp", None, "tp"),
        P("fsdp", "tp"),
        P(None, None, "ctx", "fsdp", None),
    )
    return jax.shard_map(
        on_device,
        mesh=mesh,
        in_specs=placed,
        out_specs=(
            P(None, None, "ctx", "fsdp", None),
            P(None, None, "ctx", "fsdp", None),
            P(),
            P("fsdp", "tp"),
            P("fsdp", None, "tp"),
            P("fsdp", "tp"),
            P("fsdp", None, "tp"),
            P("fsdp", "tp"),
        ),
        check_vma=False,
    )
```

profile of v0, /device:TPU:0, one launch (start us, length us, event | category | flops | bytes accessed | tf_op | source)
XLA Modules:
  0.0 1134.2 jit_solution(17363637189309043584)
XLA Ops:
  15.3 22.3 %fusion.89 = (bf16[576,1,4608]{2,1,0:T(2,128)(2,1)}, bf16[576,1,4608]{2,1,0:T(2,128)(2,1)}) fusion(bf16[576,2,4608]{2,1,0:T(2,128)(2,1)} %param.17), kind=kLoop, calls=%fused_computation.195 | loop fusion | bytes 21233664 | tf_op jit(solution)/shard_map/slice | solution.py:145
  37.6 8.0 constant_dynamic-slice_fusion.2
  55.5 53.1 %all-gather = s32[32,2,1,32]{3,1,2,0:T(2,128)S(1)} all-gather(s32[2,2,1,32]{3,1,2,0:T(2,128)S(1)} %bitcast.246), channel_id=2, replica_groups=mesh['fsdp'=4,'ctx'=4,'tp'=2] {'fsdp','ctx'}, dimensions={0}, use_global_device_ids=true | all-gather | bytes 8704 | tf_op jit(solution)/shard_map/all_gather | solution.py:161
  122.7 22.6 %collective-permute-done.6 = bf16[2,256,512]{2,1,0:T(8,128)(2,1)S(1)} collective-permute-done((bf16[2,256,512]{2,1,0:T(8,128)(2,1)S(1)}, bf16[2,256,512]{2,1,0:T(8,128)(2,1)S(1)}, u32[]{:S(2)}, u32[]{:S(2)}) %collective-permute-start.6) | collective-permute-done | bytes 524320 | tf_op jit(solution)/shard_map/ppermute | solution.py:47
  145.3 10.2 collective-permute-done.5
  179.7 7.4 collective-permute-done.10
  187.1 17.3 %collective-permute-done.9 = bf16[64,2304]{1,0:T(8,128)(2,1)S(1)} collective-permute-done((bf16[64,2304]{1,0:T(8,128)(2,1)S(1)}, bf16[64,2304]{1,0:T(8,128)(2,1)S(1)}, u32[]{:S(2)}, u32[]{:S(2)}) %collective-permute-start.9) | collective-permute-done | bytes 294944 | tf_op jit(solution)/shard_map/ppermute | solution.py:47
  209.8 7.3 collective-permute-done.13
  217.1 14.3 %collective-permute-done.12 = bf16[64,2304]{1,0:T(8,128)(2,1)S(1)} collective-permute-done((bf16[64,2304]{1,0:T(8,128)(2,1)S(1)}, bf16[64,2304]{1,0:T(8,128)(2,1)S(1)}, u32[]{:S(2)}, u32[]{:S(2)}) %collective-permute-start.12) | collective-permute-done | bytes 294944 | tf_op jit(solution)/shard_map/ppermute | solution.py:47
  234.8 9.4 fusion.98
  248.2 41.0 %all-gather.21.cloned.1.call-done = bf16[2304,1152]{1,0:T(8,128)(2,1)} async-done(((bf16[576,1152]{1,0:T(8,128)(2,1)}), bf16[2304,1152]{1,0:T(8,128)(2,1)}) %all-gather.21.cloned.1.call-update) | async-done | bytes 5308432 | tf_op jit(solution)/shard_map/all_gather | solution.py:149
  303.2 7.4 collective-permute-done.18
  310.6 17.1 %collective-permute-done.17 = bf16[64,2304]{1,0:T(8,128)(2,1)S(1)} collective-permute-done((bf16[64,2304]{1,0:T(8,128)(2,1)S(1)}, bf16[64,2304]{1,0:T(8,128)(2,1)S(1)}, u32[]{:S(2)}, u32[]{:S(2)}) %collective-permute-start.17) | collective-permute-done | bytes 294944 | tf_op jit(solution)/shard_map/ppermute | solution.py:47
  334.3 7.5 collective-permute-done.21
  341.7 14.3 %collective-permute-done.20 = bf16[64,2304]{1,0:T(8,128)(2,1)S(1)} collective-permute-done((bf16[64,2304]{1,0:T(8,128)(2,1)S(1)}, bf16[64,2304]{1,0:T(8,128)(2,1)S(1)}, u32[]{:S(2)}, u32[]{:S(2)}) %collective-permute-start.20) | collective-permute-done | bytes 294944 | tf_op jit(solution)/shard_map/ppermute | solution.py:47
  363.8 9.1 fusion.19
  380.8 7.4 collective-permute-done.26
  388.2 14.3 %collective-permute-done.25 = bf16[64,2304]{1,0:T(8,128)(2,1)S(1)} collective-permute-done((bf16[64,2304]{1,0:T(8,128)(2,1)S(1)}, bf16[64,2304]{1,0:T(8,128)(2,1)S(1)}, u32[]{:S(2)}, u32[]{:S(2)}) %collective-permute-start.25) | collective-permute-done | bytes 294944 | tf_op jit(solution)/shard_map/ppermute | solution.py:47
  409.0 7.5 collective-permute-done.29
  416.4 14.4 %collective-permute-done.28 = bf16[64,2304]{1,0:T(8,128)(2,1)S(1)} collective-permute-done((bf16[64,2304]{1,0:T(8,128)(2,1)S(1)}, bf16[64,2304]{1,0:T(8,128)(2,1)S(1)}, u32[]{:S(2)}, u32[]{:S(2)}) %collective-permute-start.28) | collective-permute-done | bytes 294944 | tf_op jit(solution)/shard_map/ppermute | solution.py:47
  453.6 22.3 %collective-permute-done.31 = bf16[2,1024,256]{2,1,0:T(8,128)(2,1)} collective-permute-done((bf16[2,1024,256]{2,1,0:T(8,128)(2,1)}, bf16[2,1024,256]{2,1,0:T(8,128)(2,1)}, u32[]{:S(2)}, u32[]{:S(2)}) %collective-permute-start.31) | collective-permute-done | bytes 1048608 | tf_op jit(solution)/shard_map/ppermute | solution.py:47
  504.3 9.8 convolution_convert_fusion
  525.4 7.4 collective-permute-done.38
  532.8 17.0 %collective-permute-done.37 = bf16[64,2304]{1,0:T(8,128)(2,1)S(1)} collective-permute-done((bf16[64,2304]{1,0:T(8,128)(2,1)S(1)}, bf16[64,2304]{1,0:T(8,128)(2,1)S(1)}, u32[]{:S(2)}, u32[]{:S(2)}) %collective-permute-start.37) | collective-permute-done | bytes 294944 | tf_op jit(solution)/shard_map/ppermute | solution.py:47
  552.6 45.3 %reduce-scatter.11.cloned.1.call-done = bf16[576,1152]{1,0:T(8,128)(2,1)} async-done(((bf16[2304,1152]{1,0:T(8,128)(2,1)}), bf16[576,1152]{1,0:T(8,128)(2,1)}) %reduce-scatter.11.cloned.1.call-update) | async-done | bytes 1327120 | tf_op jit(solution)/shard_map/reduce_scatter | solution.py:218
  598.0 108.2 %reduce-scatter.9.cloned.1.call-done = bf16[576,2304]{1,0:T(8,128)(2,1)} async-done(((bf16[2304,2304]{1,0:T(8,128)(2,1)}), bf16[576,2304]{1,0:T(8,128)(2,1)}) %reduce-scatter.9.cloned.1.call-update) | async-done | bytes 2654224 | tf_op jit(solution)/shard_map/reduce_scatter | solution.py:218
  725.4 25.3 %all-gather.27.cloned.1.call-done = bf16[2304,256]{1,0:T(8,128)(2,1)} async-done(((bf16[576,256]{1,0:T(8,128)(2,1)}), bf16[2304,256]{1,0:T(8,128)(2,1)}) %all-gather.27.cloned.1.call-update) | async-done | bytes 1179664 | tf_op jit(solution)/shard_map/all_gather | solution.py:223
  753.8 48.0 %all-gather.25.cloned.1.call-done = bf16[2304,512]{1,0:T(8,128)(2,1)} async-done(((bf16[576,512]{1,0:T(8,128)(2,1)}), bf16[2304,512]{1,0:T(8,128)(2,1)}) %all-gather.25.cloned.1.call-update) | async-done | bytes 2359312 | tf_op jit(solution)/shard_map/all_gather | solution.py:223
  810.7 90.5 %all-gather.31.cloned.1.call-done = bf16[2304,1152]{1,0:T(8,128)(2,1)} async-done(((bf16[576,1152]{1,0:T(8,128)(2,1)}), bf16[2304,1152]{1,0:T(8,128)(2,1)}) %all-gather.31.cloned.1.call-update) | async-done | bytes 5308432 | tf_op jit(solution)/shard_map/all_gather | solution.py:223
  910.9 176.4 %all-gather.29.cloned.1.call-done = bf16[2304,2304]{1,0:T(8,128)(2,1)} async-done(((bf16[576,2304]{1,0:T(8,128)(2,1)}), bf16[2304,2304]{1,0:T(8,128)(2,1)}) %all-gather.29.cloned.1.call-update) | async-done | bytes 10616848 | tf_op jit(solution)/shard_map/all_gather | solution.py:223
  1087.3 22.6 %reshape.382 = f32[4,576,2,1152]{3,2,1,0:T(2,128)} reshape(bf16[2304,2304]{1,0:T(8,128)(2,1)} %all-gather.29.cloned.1.call-done) | data formatting | bytes 31850496 | tf_op jit(solution)/shard_map/reshape | solution.py:284
  1109.9 15.5 %copy.89 = f32[4,576,1,2,1152]{4,3,0,2,1:T(2,128)} copy(f32[4,576,1,2,1152]{4,3,2,1,0:T(2,128)} %bitcast.164) | data formatting | bytes 42467328 | tf_op jit(solution)/shard_map/reshape | solution.py:284
  (371 shorter events, 218.0 us)
Async XLA Ops:
  7.2 106.4 %all-gather.15.cloned.1.call-start = ((), (), s32[]{:S(2)}) async-start(), calls=%async_computation.4 | async-start | bytes 4423680 | tf_op jit(solution)/shard_map/all_gather | solution.py:149
  13.5 150.9 %all-gather.17.cloned.1.call-start = ((), (), s32[]{:S(2)}) async-start(), calls=%async_computation.5 | async-start | bytes 1474560 | tf_op jit(solution)/shard_map/all_gather | solution.py:149
  15.3 219.5 %all-gather.19.cloned.1.call-start = ((), (), s32[]{:S(2)}) async-start(), calls=%async_computation.6 | async-start | bytes 13271040 | tf_op jit(solution)/shard_map/all_gather | solution.py:149
  47.8 241.5 %all-gather.21.cloned.1.call-start = ((), (), s32[]{:S(2)}) async-start(), calls=%async_computation.7 | async-start | bytes 6635520 | tf_op jit(solution)/shard_map/all_gather | solution.py:149
  49.8 59.1 %collective-permute-start.2 = (bf16[64,2304]{1,0:T(8,128)(2,1)S(1)}, bf16[64,2304]{1,0:T(8,128)(2,1)S(1)}, u32[]{:S(2)}, u32[]{:S(2)}) collective-permute-start(bf16[64,2304]{1,0:T(8,128)(2,1)S(1)} %fusion.49), channel_id=1, source_target_pairs={{0,6},{2,4},{4,2},{6,0},{1,7},{3,5},{5,3},{7,1},{8,14},{10,12},{12... | collective-permute-start | bytes 884744 | tf_op jit(solution)/shard_map/ppermute | solution.py:47
  54.9 54.0 %collective-permute-start.1 = (bf16[64,2304]{1,0:T(8,128)(2,1)S(1)}, bf16[64,2304]{1,0:T(8,128)(2,1)S(1)}, u32[]{:S(2)}, u32[]{:S(2)}) collective-permute-start(bf16[64,2304]{1,0:T(8,128)(2,1)S(1)} %fusion.49), channel_id=1, source_target_pairs={{0,4},{2,6},{4,0},{6,2},{1,5},{3,7},{5,1},{7,3},{8,12},{10,14},{12... | collective-permute-start | bytes 884744 | tf_op jit(solution)/shard_map/ppermute | solution.py:47
  54.9 54.0 %collective-permute-start = (bf16[64,2304]{1,0:T(8,128)(2,1)S(1)}, bf16[64,2304]{1,0:T(8,128)(2,1)S(1)}, u32[]{:S(2)}, u32[]{:S(2)}) collective-permute-start(bf16[64,2304]{1,0:T(8,128)(2,1)S(1)} %fusion.49), channel_id=1, source_target_pairs={{0,2},{2,0},{4,6},{6,4},{1,3},{3,1},{5,7},{7,5},{8,10},{10,8},{12,... | collective-permute-start | bytes 884744 | tf_op jit(solution)/shard_map/ppermute | solution.py:47
  118.3 27.0 %collective-permute-start.6 = (bf16[2,256,512]{2,1,0:T(8,128)(2,1)S(1)}, bf16[2,256,512]{2,1,0:T(8,128)(2,1)S(1)}, u32[]{:S(2)}, u32[]{:S(2)}) collective-permute-start(bf16[2,256,512]{2,1,0:T(8,128)(2,1)S(1)} %bitcast.202), channel_id=1, source_target_pairs={{0,24},{8,16},{16,8},{24,0},{1,25},{9,17},{17,9},{25,1},{2,26},{10... | collective-permute-start | bytes 1572872 | tf_op jit(solution)/shard_map/ppermute | solution.py:47
  118.4 37.1 %collective-permute-start.5 = (bf16[2,256,512]{2,1,0:T(8,128)(2,1)S(1)}, bf16[2,256,512]{2,1,0:T(8,128)(2,1)}, u32[]{:S(2)}, u32[]{:S(2)}) collective-permute-start(bf16[2,256,512]{2,1,0:T(8,128)(2,1)S(1)} %bitcast.203), channel_id=1, source_target_pairs={{0,16},{8,24},{16,0},{24,8},{1,17},{9,25},{17,1},{25,9},{2,18},{10... | collective-permute-start | bytes 1572872 | tf_op jit(solution)/shard_map/ppermute | solution.py:47
  120.1 39.6 %collective-permute-start.4 = (bf16[2,256,512]{2,1,0:T(8,128)(2,1)S(1)}, bf16[2,256,512]{2,1,0:T(8,128)(2,1)}, u32[]{:S(2)}, u32[]{:S(2)}) collective-permute-start(bf16[2,256,512]{2,1,0:T(8,128)(2,1)S(1)} %bitcast.204), channel_id=1, source_target_pairs={{0,8},{8,0},{16,24},{24,16},{1,9},{9,1},{17,25},{25,17},{2,10},{10... | collective-permute-start | bytes 1572872 | tf_op jit(solution)/shard_map/ppermute | solution.py:47
  172.8 378.4 %reduce-scatter.7.cloned.1.call-start = ((), (), s32[]{:S(2)}) async-start(), calls=%async_computation.10 | async-start | bytes 1474560 | tf_op jit(solution)/shard_map/reduce_scatter | solution.py:218
  178.8 25.6 %collective-permute-start.9 = (bf16[64,2304]{1,0:T(8,128)(2,1)S(1)}, bf16[64,2304]{1,0:T(8,128)(2,1)S(1)}, u32[]{:S(2)}, u32[]{:S(2)}) collective-permute-start(bf16[64,2304]{1,0:T(8,128)(2,1)S(1)} %get-tuple-element.80), channel_id=1, source_target_pairs={{0,4},{2,6},{4,0},{6,2},{1,5},{3,7},{5,1},{7,3},{8,12},{10,14},{12... | collective-permute-start | bytes 884744 | tf_op jit(solution)/shard_map/ppermute | solution.py:47
  178.9 25.6 %collective-permute-start.8 = (bf16[64,2304]{1,0:T(8,128)(2,1)S(1)}, bf16[64,2304]{1,0:T(8,128)(2,1)S(1)}, u32[]{:S(2)}, u32[]{:S(2)}) collective-permute-start(bf16[64,2304]{1,0:T(8,128)(2,1)S(1)} %get-tuple-element.78), channel_id=1, source_target_pairs={{0,2},{2,0},{4,6},{6,4},{1,3},{3,1},{5,7},{7,5},{8,10},{10,8},{12,... | collective-permute-start | bytes 884744 | tf_op jit(solution)/shard_map/ppermute | solution.py:47
  207.6 23.8 %collective-permute-start.12 = (bf16[64,2304]{1,0:T(8,128)(2,1)S(1)}, bf16[64,2304]{1,0:T(8,128)(2,1)S(1)}, u32[]{:S(2)}, u32[]{:S(2)}) collective-permute-start(bf16[64,2304]{1,0:T(8,128)(2,1)S(1)} %multiply_convert_fusion.4), channel_id=1, source_target_pairs={{0,4},{2,6},{4,0},{6,2},{1,5},{3,7},{5,1},{7,3},{8,12},{10,14},{12... | collective-permute-start | bytes 884744 | tf_op jit(solution)/shard_map/ppermute | solution.py:47
  207.6 23.8 %collective-permute-start.11 = (bf16[64,2304]{1,0:T(8,128)(2,1)S(1)}, bf16[64,2304]{1,0:T(8,128)(2,1)S(1)}, u32[]{:S(2)}, u32[]{:S(2)}) collective-permute-start(bf16[64,2304]{1,0:T(8,128)(2,1)S(1)} %multiply_convert_fusion.4), channel_id=1, source_target_pairs={{0,2},{2,0},{4,6},{6,4},{1,3},{3,1},{5,7},{7,5},{8,10},{10,8},{12,... | collective-permute-start | bytes 884744 | tf_op jit(solution)/shard_map/ppermute | solution.py:47
  302.2 25.6 %collective-permute-start.17 = (bf16[64,2304]{1,0:T(8,128)(2,1)S(1)}, bf16[64,2304]{1,0:T(8,128)(2,1)S(1)}, u32[]{:S(2)}, u32[]{:S(2)}) collective-permute-start(bf16[64,2304]{1,0:T(8,128)(2,1)S(1)} %get-tuple-element.77), channel_id=1, source_target_pairs={{0,4},{2,6},{4,0},{6,2},{1,5},{3,7},{5,1},{7,3},{8,12},{10,14},{12... | collective-permute-start | bytes 884744 | tf_op jit(solution)/shard_map/ppermute | solution.py:47
  302.2 25.6 %collective-permute-start.16 = (bf16[64,2304]{1,0:T(8,128)(2,1)S(1)}, bf16[64,2304]{1,0:T(8,128)(2,1)S(1)}, u32[]{:S(2)}, u32[]{:S(2)}) collective-permute-start(bf16[64,2304]{1,0:T(8,128)(2,1)S(1)} %get-tuple-element.75), channel_id=1, source_target_pairs={{0,2},{2,0},{4,6},{6,4},{1,3},{3,1},{5,7},{7,5},{8,10},{10,8},{12,... | collective-permute-start | bytes 884744 | tf_op jit(solution)/shard_map/ppermute | solution.py:47
  332.3 23.8 %collective-permute-start.20 = (bf16[64,2304]{1,0:T(8,128)(2,1)S(1)}, bf16[64,2304]{1,0:T(8,128)(2,1)S(1)}, u32[]{:S(2)}, u32[]{:S(2)}) collective-permute-start(bf16[64,2304]{1,0:T(8,128)(2,1)S(1)} %get-tuple-element.86), channel_id=1, source_target_pairs={{0,4},{2,6},{4,0},{6,2},{1,5},{3,7},{5,1},{7,3},{8,12},{10,14},{12... | collective-permute-start | bytes 884744 | tf_op jit(solution)/shard_map/ppermute | solution.py:47
  332.3 23.8 %collective-permute-start.19 = (bf16[64,2304]{1,0:T(8,128)(2,1)S(1)}, bf16[64,2304]{1,0:T(8,128)(2,1)S(1)}, u32[]{:S(2)}, u32[]{:S(2)}) collective-permute-start(bf16[64,2304]{1,0:T(8,128)(2,1)S(1)} %get-tuple-element.86), channel_id=1, source_target_pairs={{0,2},{2,0},{4,6},{6,4},{1,3},{3,1},{5,7},{7,5},{8,10},{10,8},{12,... | collective-permute-start | bytes 884744 | tf_op jit(solution)/shard_map/ppermute | solution.py:47
  377.9 24.6 %collective-permute-start.25 = (bf16[64,2304]{1,0:T(8,128)(2,1)S(1)}, bf16[64,2304]{1,0:T(8,128)(2,1)S(1)}, u32[]{:S(2)}, u32[]{:S(2)}) collective-permute-start(bf16[64,2304]{1,0:T(8,128)(2,1)S(1)} %get-tuple-element.74), channel_id=1, source_target_pairs={{0,4},{2,6},{4,0},{6,2},{1,5},{3,7},{5,1},{7,3},{8,12},{10,14},{12... | collective-permute-start | bytes 884744 | tf_op jit(solution)/shard_map/ppermute | solution.py:47
  377.9 24.6 %collective-permute-start.24 = (bf16[64,2304]{1,0:T(8,128)(2,1)S(1)}, bf16[64,2304]{1,0:T(8,128)(2,1)S(1)}, u32[]{:S(2)}, u32[]{:S(2)}) collective-permute-start(bf16[64,2304]{1,0:T(8,128)(2,1)S(1)} %get-tuple-element.72), channel_id=1, source_target_pairs={{0,2},{2,0},{4,6},{6,4},{1,3},{3,1},{5,7},{7,5},{8,10},{10,8},{12,... | collective-permute-start | bytes 884744 | tf_op jit(solution)/shard_map/ppermute | solution.py:47
  450.4 25.5 %collective-permute-start.31 = (bf16[2,1024,256]{2,1,0:T(8,128)(2,1)}, bf16[2,1024,256]{2,1,0:T(8,128)(2,1)}, u32[]{:S(2)}, u32[]{:S(2)}) collective-permute-start(bf16[2,1024,256]{2,1,0:T(8,128)(2,1)} %bitcast.221), channel_id=1, source_target_pairs={{0,2},{2,0},{4,6},{6,4},{1,3},{3,1},{5,7},{7,5},{8,10},{10,8},{12,... | collective-permute-start | bytes 3145736 | tf_op jit(solution)/shard_map/ppermute | solution.py:47
  453.5 98.3 %reduce-scatter.5.cloned.1.call-start = ((), (), s32[]{:S(2)}) async-start(), calls=%async_computation.9 | async-start | bytes 2949120 | tf_op jit(solution)/shard_map/reduce_scatter | solution.py:218
  495.7 102.2 %reduce-scatter.11.cloned.1.call-start = ((), (), s32[]{:S(2)}) async-start(), calls=%async_computation.12 | async-start | bytes 6635520 | tf_op jit(solution)/shard_map/reduce_scatter | solution.py:218
  502.3 203.9 %reduce-scatter.9.cloned.1.call-start = ((), (), s32[]{:S(2)}) async-start(), calls=%async_computation.11 | async-start | bytes 13271040 | tf_op jit(solution)/shard_map/reduce_scatter | solution.py:218
  514.1 211.3 %all-gather.23.cloned.1.call-start = ((), (), s32[]{:S(2)}) async-start(), calls=%async_computation.8 | async-start | bytes 1769472 | tf_op jit(solution)/shard_map/all_gather | solution.py:270
  523.6 26.2 %collective-permute-start.37 = (bf16[64,2304]{1,0:T(8,128)(2,1)S(1)}, bf16[64,2304]{1,0:T(8,128)(2,1)S(1)}, u32[]{:S(2)}, u32[]{:S(2)}) collective-permute-start(bf16[64,2304]{1,0:T(8,128)(2,1)S(1)} %get-tuple-element.71), channel_id=1, source_target_pairs={{0,4},{2,6},{4,0},{6,2},{1,5},{3,7},{5,1},{7,3},{8,12},{10,14},{12... | collective-permute-start | bytes 884744 | tf_op jit(solution)/shard_map/ppermute | solution.py:47
  523.7 26.0 %collective-permute-start.36 = (bf16[64,2304]{1,0:T(8,128)(2,1)S(1)}, bf16[64,2304]{1,0:T(8,128)(2,1)S(1)}, u32[]{:S(2)}, u32[]{:S(2)}) collective-permute-start(bf16[64,2304]{1,0:T(8,128)(2,1)S(1)} %get-tuple-element.69), channel_id=1, source_target_pairs={{0,2},{2,0},{4,6},{6,4},{1,3},{3,1},{5,7},{7,5},{8,10},{10,8},{12,... | collective-permute-start | bytes 884744 | tf_op jit(solution)/shard_map/ppermute | solution.py:47
  551.2 199.5 %all-gather.27.cloned.1.call-start = ((), (), s32[]{:S(2)}) async-start(), calls=%async_computation.14 | async-start | bytes 1474560 | tf_op jit(solution)/shard_map/all_gather | solution.py:223
  551.8 250.1 %all-gather.25.cloned.1.call-start = ((), (), s32[]{:S(2)}) async-start(), calls=%async_computation.13 | async-start | bytes 2949120 | tf_op jit(solution)/shard_map/all_gather | solution.py:223
  552.5 348.7 %all-gather.31.cloned.1.call-start = ((), (), s32[]{:S(2)}) async-start(), calls=%async_computation.16 | async-start | bytes 6635520 | tf_op jit(solution)/shard_map/all_gather | solution.py:223
  597.9 489.4 %all-gather.29.cloned.1.call-start = ((), (), s32[]{:S(2)}) async-start(), calls=%async_computation.15 | async-start | bytes 13271040 | tf_op jit(solution)/shard_map/all_gather | solution.py:223
  (92 other events, 1947.3 us)
Sparse Core Ops, SparseCore 0:
  13.6 49.9 all-gather.14
  66.0 27.8 all-gather.16
  96.3 128.5 all-gather.18
  227.2 61.9 all-gather.20
  453.6 27.2 reduce-scatter.6
  495.8 36.4 reduce-scatter.4
  535.9 61.9 reduce-scatter.10
  601.6 104.5 reduce-scatter.8
  708.3 9.2 all-gather.22
  719.0 31.5 all-gather.26
  752.2 49.5 all-gather.24
  803.3 97.9 all-gather.30
  902.8 184.4 all-gather.28
where the time goes:
time: 1140 us; the launch traced here: 1130 us
  waiting for transfers between devices  793 us (70%)
  local copies, waits for them, and re-layouts  120 us (11%)
  matrix products  66.1 us (6%)
  blocking collectives  55.4 us (5%)
  starting transfers between devices  52.4 us (5%)
  other arithmetic  30.8 us (3%)
  between operations  15.7 us (1%)
    all_gather x4, waiting for transfers between devices, spread(): return lax.all_gather(part, 'ctx', axis=0, tiled=False)  340 us
    ppermute x44, waiting for transfers between devices, swap(): lax.ppermute(values, axis_name, [(i, i ^ offset) for i in range(count)])  257 us
    reduce_scatter x4, waiting for transfers between devices, weight_grad(): lax.psum_scatter(dot_tn(left, right).astype(BF16), 'fsdp', scatter_dimens...  154 us
    all_gather x1, blocking collectives, on_device(): lax.all_gather(segments.reshape(seq_count, 2, half_dev), ('fsdp', 'ctx'),...  53.1 us
    ppermute x44, starting transfers between devices, swap(): lax.ppermute(values, axis_name, [(i, i ^ offset) for i in range(count)])  51.7 us
    all_gather x4, waiting for transfers between devices, on_device(): lax.all_gather(part, 'fsdp', axis=0, tiled=True)  41 us
    reshape x2, local copies, waits for them, and re-layouts, on_device(): columns(all_in.reshape(ctx_count, own_width, 2, ff_width))  38.1 us
  transfers between devices with their start and end apart: 57, of which 40 were waited for; matrix products, arithmetic and copies ran while one was open for 10% of the time, Pallas kernels for 0%

commit v1 on v0

--- a/solution.py
+++ b/solution.py
@@ -8,6 +8,28 @@
 NORM_EPS = 1e-06
 F32 = jnp.float32
 BF16 = jnp.bfloat16
+
+
+def in_order(blocks, dim):
+    dims = list(blocks.shape[1:])
+    dims[dim] *= blocks.shape[0]
+    return jnp.moveaxis(blocks, 0, dim).reshape(dims)
+
+
+def ring_gather(x, axis, dim):
+    size = lax.axis_size(axis)
+    pairs = [(i, (i + 1) % size) for i in range(size)]
+    back = [(b, a) for a, b in pairs]
+    lower, upper = ([], [])
+    for lap in range(size - 1):
+        if lap % 2 == 0:
+            lower.append(lax.ppermute(lower[-1] if lower else x, axis, pairs))
+        else:
+            upper.append(lax.ppermute(upper[-1] if upper else x, axis, back))
+    blocks = jnp.stack([*lower[::-1], x, *upper])
+    shift = lax.axis_index(axis) - len(lower)
+    blocks = blocks[(jnp.arange(size) - shift) % size]
+    return in_order(blocks, dim)
 
 
 def rms_factor(values):
@@ -146,8 +168,7 @@
     )
     out_part = cols(ffn_out, ff_at, ff_width)
     w_qkv, w_attn, w_in, w_out = (
-        lax.all_gather(part, "fsdp", axis=0, tiled=True)
-        for part in (qkv_part, attn_part, in_part, out_part)
+        ring_gather(part, "fsdp", 0) for part in (qkv_part, attn_part, in_part, out_part)
     )
     gain_pre, gain_post, gain_ffn, gain_last = (norm_gains[i] for i in range(4))
     row_at = tp_at * own_count

time: 1140 us -> 1190 us (1.044)
  other arithmetic: 30.8 us -> 62.2 us
  local copies, waits for them, and re-layouts: 120 us -> 149 us
    ppermute x0 -> x12, waiting for transfers between devices: none -> 249 us  [the longest x8 175 us: ring_gather(): lower.append(lax.ppermute(lower[-1] if lower else x, axis, pairs))]
    all_gather x4, waiting for transfers between devices: 340 us -> 178 us  [spread(): return lax.all_gather(part, 'ctx', axis=0, tiled=False)]
    ppermute x44, waiting for transfers between devices: 257 us -> 202 us  [swap(): lax.ppermute(values, axis_name, [(i, i ^ offset) for i in range(count)])]
    all_gather x4 -> x0, waiting for transfers between devices: 41 us -> none  [on_device(): lax.all_gather(part, 'fsdp', axis=0, tiled=True)]
    gather x0 -> x6, local copies, waits for them, and re-layouts: none -> 32.1 us  [ring_gather(): blocks = blocks[(jnp.arange(size) - shift) % size]]
    another operation x5 -> x11, other arithmetic: 2.82 us -> 22.8 us  [the longest x6 20 us: ring_gather(): blocks = jnp.stack([*lower[::-1], x, *upper])]
    ppermute x0 -> x12, starting transfers between devices: none -> 15 us  [the longest x8 9.48 us: ring_gather(): lower.append(lax.ppermute(lower[-1] if lower else x, axis, pairs))]
  transfers between devices with their start and end apart: 57 -> 65, of which waited for: 40 -> 36; matrix products, arithmetic and copies ran while one was open for 10% -> 11% of each run, Pallas kernels for 0% -> 0%
where the time goes in v1:
time: 1190 us; the launch traced here: 1180 us
  waiting for transfers between devices  784 us (66%)
  local copies, waits for them, and re-layouts  149 us (13%)
  other arithmetic  62.2 us (5%)
  starting transfers between devices  62 us (5%)
  matrix products  58.8 us (5%)
  blocking collectives  45.9 us (4%)
  between operations  17.1 us (1%)
    ppermute x44, waiting for transfers between devices, swap(): lax.ppermute(values, axis_name, [(i, i ^ offset) for i in range(count)])  202 us
    all_gather x4, waiting for transfers between devices, spread(): return lax.all_gather(part, 'ctx', axis=0, tiled=False)  178 us
    ppermute x8, waiting for transfers between devices, ring_gather(): lower.append(lax.ppermute(lower[-1] if lower else x, axis, pairs))  175 us
    reduce_scatter x4, waiting for transfers between devices, weight_grad(): lax.psum_scatter(dot_tn(left, right).astype(BF16), 'fsdp', scatter_dimens...  155 us
    ppermute x4, waiting for transfers between devices, ring_gather(): upper.append(lax.ppermute(upper[-1] if upper else x, axis, back))  74.3 us
    ppermute x44, starting transfers between devices, swap(): lax.ppermute(values, axis_name, [(i, i ^ offset) for i in range(count)])  46.3 us
    all_gather x1, blocking collectives, on_device(): lax.all_gather(segments.reshape(seq_count, 2, half_dev), ('fsdp', 'ctx'),...  43.3 us
    reshape x2, local copies, waits for them, and re-layouts, on_device(): columns(all_in.reshape(ctx_count, own_width, 2, ff_width))  38.1 us
  transfers between devices with their start and end apart: 65, of which 36 were waited for; matrix products, arithmetic and copies ran while one was open for 11% of the time, Pallas kernels for 0%

profile of v1, /device:TPU:0, one launch (start us, length us, event | category | flops | bytes accessed | tf_op | source)
XLA Modules:
  0.0 1178.9 jit_solution(4719960250197498318)
XLA Ops:
  28.7 43.3 %all-gather = s32[32,2,1,32]{3,1,2,0:T(2,128)S(1)} all-gather(s32[2,2,1,32]{3,1,2,0:T(2,128)S(1)} %bitcast.282), channel_id=2, replica_groups=mesh['fsdp'=4,'ctx'=4,'tp'=2] {'fsdp','ctx'}, dimensions={0}, use_global_device_ids=true | all-gather | bytes 8704 | tf_op jit(solution)/shard_map/all_gather | solution.py:182
  73.2 22.3 %fusion.94 = (bf16[576,1,4608]{2,1,0:T(2,128)(2,1)}, bf16[576,1,4608]{2,1,0:T(2,128)(2,1)}) fusion(bf16[576,2,4608]{2,1,0:T(2,128)(2,1)} %param.17), kind=kLoop, calls=%fused_computation.215 | loop fusion | bytes 21233664 | tf_op jit(solution)/shard_map/slice | solution.py:167
  105.0 20.8 %collective-permute-done.5 = bf16[576,768]{1,0:T(8,128)(2,1)} collective-permute-done((bf16[576,768]{1,0:T(8,128)(2,1)}, bf16[576,768]{1,0:T(8,128)(2,1)}, u32[]{:S(2)}, u32[]{:S(2)}) %collective-permute-start.5) | collective-permute-done | bytes 884768 | tf_op jit(solution)/shard_map/ppermute | solution.py:26
  144.5 23.2 %collective-permute-done.11 = bf16[576,256]{1,0:T(8,128)(2,1)S(1)} collective-permute-done((bf16[576,256]{1,0:T(8,128)(2,1)}, bf16[576,256]{1,0:T(8,128)(2,1)S(1)}, u32[]{:S(2)}, u32[]{:S(2)}) %collective-permute-start.11) | collective-permute-done | bytes 294944 | tf_op jit(solution)/shard_map/ppermute | solution.py:26
  176.9 8.0 constant_dynamic-slice_fusion.2
  200.2 16.7 %collective-permute-done.15 = bf16[64,2304]{1,0:T(8,128)(2,1)S(1)} collective-permute-done((bf16[64,2304]{1,0:T(8,128)(2,1)S(1)}, bf16[64,2304]{1,0:T(8,128)(2,1)S(1)}, u32[]{:S(2)}, u32[]{:S(2)}) %collective-permute-start.15) | collective-permute-done | bytes 294944 | tf_op jit(solution)/shard_map/ppermute | solution.py:69
  221.5 56.4 %collective-permute-done.24 = bf16[576,1152]{1,0:T(8,128)(2,1)S(1)} collective-permute-done((bf16[576,1152]{1,0:T(8,128)(2,1)S(1)}, bf16[576,1152]{1,0:T(8,128)(2,1)S(1)}, u32[]{:S(2)}, u32[]{:S(2)}) %collective-permute-start.24) | collective-permute-done | bytes 1327136 | tf_op jit(solution)/shard_map/ppermute | solution.py:26
  281.1 7.6 collective-permute-done.17
  289.0 74.3 %collective-permute-done.26 = bf16[576,1152]{1,0:T(8,128)(2,1)S(1)} collective-permute-done((bf16[576,1152]{1,0:T(8,128)(2,1)S(1)}, bf16[576,1152]{1,0:T(8,128)(2,1)S(1)}, u32[]{:S(2)}, u32[]{:S(2)}) %collective-permute-start.26) | collective-permute-done | bytes 1327136 | tf_op jit(solution)/shard_map/ppermute | solution.py:28
  363.3 28.4 %collective-permute-done.25 = bf16[576,1152]{1,0:T(8,128)(2,1)S(1)} collective-permute-done((bf16[576,1152]{1,0:T(8,128)(2,1)S(1)}, bf16[576,1152]{1,0:T(8,128)(2,1)S(1)}, u32[]{:S(2)}, u32[]{:S(2)}) %collective-permute-start.25) | collective-permute-done | bytes 1327136 | tf_op jit(solution)/shard_map/ppermute | solution.py:26
  402.3 46.0 %collective-permute-done.22 = bf16[576,2304]{1,0:T(8,128)(2,1)} collective-permute-done((bf16[576,2304]{1,0:T(8,128)(2,1)}, bf16[576,2304]{1,0:T(8,128)(2,1)}, u32[]{:S(2)}, u32[]{:S(2)}) %collective-permute-start.22) | collective-permute-done | bytes 2654240 | tf_op jit(solution)/shard_map/ppermute | solution.py:26
  448.3 8.5 pad_maximum_fusion
  456.8 9.0 fusion.93
  477.7 7.0 pad_maximum_fusion.1
  502.4 7.4 collective-permute-done.30
  509.8 16.3 %collective-permute-done.29 = bf16[64,2304]{1,0:T(8,128)(2,1)S(1)} collective-permute-done((bf16[64,2304]{1,0:T(8,128)(2,1)S(1)}, bf16[64,2304]{1,0:T(8,128)(2,1)S(1)}, u32[]{:S(2)}, u32[]{:S(2)}) %collective-permute-start.29) | collective-permute-done | bytes 294944 | tf_op jit(solution)/shard_map/ppermute | solution.py:69
  532.7 7.5 collective-permute-done.33
  540.1 13.5 %collective-permute-done.32 = bf16[64,2304]{1,0:T(8,128)(2,1)S(1)} collective-permute-done((bf16[64,2304]{1,0:T(8,128)(2,1)S(1)}, bf16[64,2304]{1,0:T(8,128)(2,1)S(1)}, u32[]{:S(2)}, u32[]{:S(2)}) %collective-permute-start.32) | collective-permute-done | bytes 294944 | tf_op jit(solution)/shard_map/ppermute | solution.py:69
  562.5 8.8 fusion.19
  582.5 7.4 collective-permute-done.38
  589.9 15.2 %collective-permute-done.37 = bf16[64,2304]{1,0:T(8,128)(2,1)S(1)} collective-permute-done((bf16[64,2304]{1,0:T(8,128)(2,1)S(1)}, bf16[64,2304]{1,0:T(8,128)(2,1)S(1)}, u32[]{:S(2)}, u32[]{:S(2)}) %collective-permute-start.37) | collective-permute-done | bytes 294944 | tf_op jit(solution)/shard_map/ppermute | solution.py:69
  611.5 7.5 collective-permute-done.41
  619.0 13.5 %collective-permute-done.40 = bf16[64,2304]{1,0:T(8,128)(2,1)S(1)} collective-permute-done((bf16[64,2304]{1,0:T(8,128)(2,1)S(1)}, bf16[64,2304]{1,0:T(8,128)(2,1)S(1)}, u32[]{:S(2)}, u32[]{:S(2)}) %collective-permute-start.40) | collective-permute-done | bytes 294944 | tf_op jit(solution)/shard_map/ppermute | solution.py:69
  656.1 21.9 %collective-permute-done.43 = bf16[2,1024,256]{2,1,0:T(8,128)(2,1)} collective-permute-done((bf16[2,1024,256]{2,1,0:T(8,128)(2,1)}, bf16[2,1024,256]{2,1,0:T(8,128)(2,1)}, u32[]{:S(2)}, u32[]{:S(2)}) %collective-permute-start.43) | collective-permute-done | bytes 1048608 | tf_op jit(solution)/shard_map/ppermute | solution.py:69
  705.5 9.6 convolution_convert_fusion
  726.5 7.4 collective-permute-done.50
  733.9 17.2 %collective-permute-done.49 = bf16[64,2304]{1,0:T(8,128)(2,1)S(1)} collective-permute-done((bf16[64,2304]{1,0:T(8,128)(2,1)S(1)}, bf16[64,2304]{1,0:T(8,128)(2,1)S(1)}, u32[]{:S(2)}, u32[]{:S(2)}) %collective-permute-start.49) | collective-permute-done | bytes 294944 | tf_op jit(solution)/shard_map/ppermute | solution.py:69
  753.8 46.3 %reduce-scatter.11.cloned.1.call-done = bf16[576,1152]{1,0:T(8,128)(2,1)} async-done(((bf16[2304,1152]{1,0:T(8,128)(2,1)}), bf16[576,1152]{1,0:T(8,128)(2,1)}) %reduce-scatter.11.cloned.1.call-update) | async-done | bytes 1327120 | tf_op jit(solution)/shard_map/reduce_scatter | solution.py:239
  800.1 108.2 %reduce-scatter.9.cloned.1.call-done = bf16[576,2304]{1,0:T(8,128)(2,1)} async-done(((bf16[2304,2304]{1,0:T(8,128)(2,1)}), bf16[576,2304]{1,0:T(8,128)(2,1)}) %reduce-scatter.9.cloned.1.call-update) | async-done | bytes 2654224 | tf_op jit(solution)/shard_map/reduce_scatter | solution.py:239
  955.0 176.3 %all-gather.17.cloned.1.call-done = bf16[2304,2304]{1,0:T(8,128)(2,1)} async-done(((bf16[576,2304]{1,0:T(8,128)(2,1)}), bf16[2304,2304]{1,0:T(8,128)(2,1)}) %all-gather.17.cloned.1.call-update) | async-done | bytes 10616848 | tf_op jit(solution)/shard_map/all_gather | solution.py:244
  1131.3 22.6 %reshape.447 = f32[4,576,2,1152]{3,2,1,0:T(2,128)} reshape(bf16[2304,2304]{1,0:T(8,128)(2,1)} %all-gather.17.cloned.1.call-done) | data formatting | bytes 31850496 | tf_op jit(solution)/shard_map/reshape | solution.py:305
  1153.9 15.5 %copy.89 = f32[4,576,1,2,1152]{4,3,0,2,1:T(2,128)} copy(f32[4,576,1,2,1152]{4,3,2,1,0:T(2,128)} %bitcast.190) | data formatting | bytes 42467328 | tf_op jit(solution)/shard_map/reshape | solution.py:305
  (408 shorter events, 268.3 us)
Async XLA Ops:
  8.0 744.6 %reduce-scatter.7.cloned.1.call-start = ((), (), s32[]{:S(2)}) async-start(), calls=%async_computation.6 | async-start | bytes 1474560 | tf_op jit(solution)/shard_map/reduce_scatter | solution.py:239
  12.7 82.9 %collective-permute-start.2 = (bf16[64,2304]{1,0:T(8,128)(2,1)}, bf16[64,2304]{1,0:T(8,128)(2,1)}, u32[]{:S(2)}, u32[]{:S(2)}) collective-permute-start(bf16[64,2304]{1,0:T(8,128)(2,1)} %fusion.49), channel_id=1, source_target_pairs={{0,6},{2,4},{4,2},{6,0},{1,7},{3,5},{5,3},{7,1},{8,14},{10,12},{12... | collective-permute-start | bytes 884744 | tf_op jit(solution)/shard_map/ppermute | solution.py:69
  17.7 77.9 %collective-permute-start.1 = (bf16[64,2304]{1,0:T(8,128)(2,1)}, bf16[64,2304]{1,0:T(8,128)(2,1)}, u32[]{:S(2)}, u32[]{:S(2)}) collective-permute-start(bf16[64,2304]{1,0:T(8,128)(2,1)} %fusion.49), channel_id=1, source_target_pairs={{0,4},{2,6},{4,0},{6,2},{1,5},{3,7},{5,1},{7,3},{8,12},{10,14},{12... | collective-permute-start | bytes 884744 | tf_op jit(solution)/shard_map/ppermute | solution.py:69
  17.7 79.9 %collective-permute-start = (bf16[64,2304]{1,0:T(8,128)(2,1)}, bf16[64,2304]{1,0:T(8,128)(2,1)}, u32[]{:S(2)}, u32[]{:S(2)}) collective-permute-start(bf16[64,2304]{1,0:T(8,128)(2,1)} %fusion.49), channel_id=1, source_target_pairs={{0,2},{2,0},{4,6},{6,4},{1,3},{3,1},{5,7},{7,5},{8,10},{10,8},{12,... | collective-permute-start | bytes 884744 | tf_op jit(solution)/shard_map/ppermute | solution.py:69
  25.9 79.1 %collective-permute-start.6 = (bf16[576,768]{1,0:T(8,128)(2,1)}, bf16[576,768]{1,0:T(8,128)(2,1)}, u32[]{:S(2)}, u32[]{:S(2)}) collective-permute-start(bf16[576,768]{1,0:T(8,128)(2,1)} %get-tuple-element.91), channel_id=1, source_target_pairs={{8,0},{16,8},{24,16},{0,24},{9,1},{17,9},{25,17},{1,25},{10,2},{18... | collective-permute-start | bytes 2654216 | tf_op jit(solution)/shard_map/ppermute | solution.py:28
  28.6 70.5 %collective-permute-start.4 = (bf16[576,768]{1,0:T(8,128)(2,1)}, bf16[576,768]{1,0:T(8,128)(2,1)}, u32[]{:S(2)}, u32[]{:S(2)}) collective-permute-start(bf16[576,768]{1,0:T(8,128)(2,1)} %get-tuple-element.91), channel_id=1, source_target_pairs={{0,8},{8,16},{16,24},{24,0},{1,9},{9,17},{17,25},{25,1},{2,10},{10... | collective-permute-start | bytes 2654216 | tf_op jit(solution)/shard_map/ppermute | solution.py:26
  95.6 48.9 %collective-permute-start.12 = (bf16[576,256]{1,0:T(8,128)(2,1)}, bf16[576,256]{1,0:T(8,128)(2,1)}, u32[]{:S(2)}, u32[]{:S(2)}) collective-permute-start(bf16[576,256]{1,0:T(8,128)(2,1)} %constant_dynamic-slice_fusion.4), channel_id=1, source_target_pairs={{8,0},{16,8},{24,16},{0,24},{9,1},{17,9},{25,17},{1,25},{10,2},{18... | collective-permute-start | bytes 884744 | tf_op jit(solution)/shard_map/ppermute | solution.py:28
  95.6 47.3 %collective-permute-start.10 = (bf16[576,256]{1,0:T(8,128)(2,1)}, bf16[576,256]{1,0:T(8,128)(2,1)}, u32[]{:S(2)}, u32[]{:S(2)}) collective-permute-start(bf16[576,256]{1,0:T(8,128)(2,1)} %constant_dynamic-slice_fusion.4), channel_id=1, source_target_pairs={{0,8},{8,16},{16,24},{24,0},{1,9},{9,17},{17,25},{25,1},{2,10},{10... | collective-permute-start | bytes 884744 | tf_op jit(solution)/shard_map/ppermute | solution.py:26
  99.1 26.6 %collective-permute-start.5 = (bf16[576,768]{1,0:T(8,128)(2,1)}, bf16[576,768]{1,0:T(8,128)(2,1)}, u32[]{:S(2)}, u32[]{:S(2)}) collective-permute-start(bf16[576,768]{1,0:T(8,128)(2,1)} %collective-permute-done.4), channel_id=1, source_target_pairs={{0,8},{8,16},{16,24},{24,0},{1,9},{9,17},{17,25},{25,1},{2,10},{10... | collective-permute-start | bytes 2654216 | tf_op jit(solution)/shard_map/ppermute | solution.py:26
  138.3 32.4 %collective-permute-start.9 = (bf16[2,256,512]{2,1,0:T(8,128)(2,1)S(1)}, bf16[2,256,512]{2,1,0:T(8,128)(2,1)}, u32[]{:S(2)}, u32[]{:S(2)}) collective-permute-start(bf16[2,256,512]{2,1,0:T(8,128)(2,1)S(1)} %bitcast.236), channel_id=1, source_target_pairs={{0,24},{8,16},{16,8},{24,0},{1,25},{9,17},{17,9},{25,1},{2,26},{10... | collective-permute-start | bytes 1572872 | tf_op jit(solution)/shard_map/ppermute | solution.py:69
  138.4 32.3 %collective-permute-start.8 = (bf16[2,256,512]{2,1,0:T(8,128)(2,1)S(1)}, bf16[2,256,512]{2,1,0:T(8,128)(2,1)}, u32[]{:S(2)}, u32[]{:S(2)}) collective-permute-start(bf16[2,256,512]{2,1,0:T(8,128)(2,1)S(1)} %bitcast.237), channel_id=1, source_target_pairs={{0,16},{8,24},{16,0},{24,8},{1,17},{9,25},{17,1},{25,9},{2,18},{10... | collective-permute-start | bytes 1572872 | tf_op jit(solution)/shard_map/ppermute | solution.py:69
  139.0 31.8 %collective-permute-start.7 = (bf16[2,256,512]{2,1,0:T(8,128)(2,1)S(1)}, bf16[2,256,512]{2,1,0:T(8,128)(2,1)}, u32[]{:S(2)}, u32[]{:S(2)}) collective-permute-start(bf16[2,256,512]{2,1,0:T(8,128)(2,1)S(1)} %bitcast.238), channel_id=1, source_target_pairs={{0,8},{8,0},{16,24},{24,16},{1,9},{9,1},{17,25},{25,17},{2,10},{10... | collective-permute-start | bytes 1572872 | tf_op jit(solution)/shard_map/ppermute | solution.py:69
  188.0 90.1 %collective-permute-start.21 = (bf16[576,2304]{1,0:T(8,128)(2,1)}, bf16[576,2304]{1,0:T(8,128)(2,1)}, u32[]{:S(2)}, u32[]{:S(2)}) collective-permute-start(bf16[576,2304]{1,0:T(8,128)(2,1)} %get-tuple-element.70), channel_id=1, source_target_pairs={{0,8},{8,16},{16,24},{24,0},{1,9},{9,17},{17,25},{25,1},{2,10},{10... | collective-permute-start | bytes 7962632 | tf_op jit(solution)/shard_map/ppermute | solution.py:26
  188.8 28.1 %collective-permute-start.15 = (bf16[64,2304]{1,0:T(8,128)(2,1)S(1)}, bf16[64,2304]{1,0:T(8,128)(2,1)S(1)}, u32[]{:S(2)}, u32[]{:S(2)}) collective-permute-start(bf16[64,2304]{1,0:T(8,128)(2,1)S(1)} %get-tuple-element.84), channel_id=1, source_target_pairs={{0,4},{2,6},{4,0},{6,2},{1,5},{3,7},{5,1},{7,3},{8,12},{10,14},{12... | collective-permute-start | bytes 884744 | tf_op jit(solution)/shard_map/ppermute | solution.py:69
  190.6 26.4 %collective-permute-start.14 = (bf16[64,2304]{1,0:T(8,128)(2,1)S(1)}, bf16[64,2304]{1,0:T(8,128)(2,1)S(1)}, u32[]{:S(2)}, u32[]{:S(2)}) collective-permute-start(bf16[64,2304]{1,0:T(8,128)(2,1)S(1)} %get-tuple-element.82), channel_id=1, source_target_pairs={{0,2},{2,0},{4,6},{6,4},{1,3},{3,1},{5,7},{7,5},{8,10},{10,8},{12,... | collective-permute-start | bytes 884744 | tf_op jit(solution)/shard_map/ppermute | solution.py:69
  192.9 85.0 %collective-permute-start.24 = (bf16[576,1152]{1,0:T(8,128)(2,1)S(1)}, bf16[576,1152]{1,0:T(8,128)(2,1)S(1)}, u32[]{:S(2)}, u32[]{:S(2)}) collective-permute-start(bf16[576,1152]{1,0:T(8,128)(2,1)S(1)} %constant_dynamic-slice_fusion.1), channel_id=1, source_target_pairs={{0,8},{8,16},{16,24},{24,0},{1,9},{9,17},{17,25},{25,1},{2,10},{10... | collective-permute-start | bytes 3981320 | tf_op jit(solution)/shard_map/ppermute | solution.py:26
  217.6 62.3 %collective-permute-start.19 = (bf16[64,2304]{1,0:T(8,128)(2,1)S(1)}, bf16[64,2304]{1,0:T(8,128)(2,1)S(1)}, u32[]{:S(2)}, u32[]{:S(2)}) collective-permute-start(bf16[64,2304]{1,0:T(8,128)(2,1)S(1)} %multiply_convert_fusion.4), channel_id=1, source_target_pairs={{0,6},{2,4},{4,2},{6,0},{1,7},{3,5},{5,3},{7,1},{8,14},{10,12},{12... | collective-permute-start | bytes 884744 | tf_op jit(solution)/shard_map/ppermute | solution.py:69
  218.9 62.1 %collective-permute-start.18 = (bf16[64,2304]{1,0:T(8,128)(2,1)S(1)}, bf16[64,2304]{1,0:T(8,128)(2,1)S(1)}, u32[]{:S(2)}, u32[]{:S(2)}) collective-permute-start(bf16[64,2304]{1,0:T(8,128)(2,1)S(1)} %multiply_convert_fusion.4), channel_id=1, source_target_pairs={{0,4},{2,6},{4,0},{6,2},{1,5},{3,7},{5,1},{7,3},{8,12},{10,14},{12... | collective-permute-start | bytes 884744 | tf_op jit(solution)/shard_map/ppermute | solution.py:69
  218.9 183.4 %collective-permute-start.23 = (bf16[576,2304]{1,0:T(8,128)(2,1)}, bf16[576,2304]{1,0:T(8,128)(2,1)}, u32[]{:S(2)}, u32[]{:S(2)}) collective-permute-start(bf16[576,2304]{1,0:T(8,128)(2,1)} %get-tuple-element.70), channel_id=1, source_target_pairs={{8,0},{16,8},{24,16},{0,24},{9,1},{17,9},{25,17},{1,25},{10,2},{18... | collective-permute-start | bytes 7962632 | tf_op jit(solution)/shard_map/ppermute | solution.py:28
  277.9 85.4 %collective-permute-start.26 = (bf16[576,1152]{1,0:T(8,128)(2,1)S(1)}, bf16[576,1152]{1,0:T(8,128)(2,1)S(1)}, u32[]{:S(2)}, u32[]{:S(2)}) collective-permute-start(bf16[576,1152]{1,0:T(8,128)(2,1)S(1)} %constant_dynamic-slice_fusion.1), channel_id=1, source_target_pairs={{8,0},{16,8},{24,16},{0,24},{9,1},{17,9},{25,17},{1,25},{10,2},{18... | collective-permute-start | bytes 3981320 | tf_op jit(solution)/shard_map/ppermute | solution.py:28
  278.1 113.6 %collective-permute-start.25 = (bf16[576,1152]{1,0:T(8,128)(2,1)S(1)}, bf16[576,1152]{1,0:T(8,128)(2,1)S(1)}, u32[]{:S(2)}, u32[]{:S(2)}) collective-permute-start(bf16[576,1152]{1,0:T(8,128)(2,1)S(1)} %collective-permute-done.24), channel_id=1, source_target_pairs={{0,8},{8,16},{16,24},{24,0},{1,9},{9,17},{17,25},{25,1},{2,10},{10... | collective-permute-start | bytes 3981320 | tf_op jit(solution)/shard_map/ppermute | solution.py:26
  280.0 168.3 %collective-permute-start.22 = (bf16[576,2304]{1,0:T(8,128)(2,1)}, bf16[576,2304]{1,0:T(8,128)(2,1)}, u32[]{:S(2)}, u32[]{:S(2)}) collective-permute-start(bf16[576,2304]{1,0:T(8,128)(2,1)} %collective-permute-done.21), channel_id=1, source_target_pairs={{0,8},{8,16},{16,24},{24,0},{1,9},{9,17},{17,25},{25,1},{2,10},{10... | collective-permute-start | bytes 7962632 | tf_op jit(solution)/shard_map/ppermute | solution.py:26
  288.8 111.9 %collective-permute-start.20 = (bf16[256,2304]{1,0:T(8,128)(2,1)S(1)}, bf16[256,2304]{1,0:T(8,128)(2,1)S(1)}, u32[]{:S(2)}, u32[]{:S(2)}) collective-permute-start(bf16[256,2304]{1,0:T(8,128)(2,1)S(1)} %bitcast.220), channel_id=1, source_target_pairs={{0,1},{1,0},{2,3},{3,2},{4,5},{5,4},{6,7},{7,6},{8,9},{9,8},{10,11... | collective-permute-start | bytes 3538952 | tf_op jit(solution)/shard_map/ppermute | solution.py:69
  498.1 28.1 %collective-permute-start.29 = (bf16[64,2304]{1,0:T(8,128)(2,1)S(1)}, bf16[64,2304]{1,0:T(8,128)(2,1)S(1)}, u32[]{:S(2)}, u32[]{:S(2)}) collective-permute-start(bf16[64,2304]{1,0:T(8,128)(2,1)S(1)} %get-tuple-element.81), channel_id=1, source_target_pairs={{0,4},{2,6},{4,0},{6,2},{1,5},{3,7},{5,1},{7,3},{8,12},{10,14},{12... | collective-permute-start | bytes 884744 | tf_op jit(solution)/shard_map/ppermute | solution.py:69
  655.7 97.5 %reduce-scatter.5.cloned.1.call-start = ((), (), s32[]{:S(2)}) async-start(), calls=%async_computation.5 | async-start | bytes 2949120 | tf_op jit(solution)/shard_map/reduce_scatter | solution.py:239
  696.9 103.1 %reduce-scatter.11.cloned.1.call-start = ((), (), s32[]{:S(2)}) async-start(), calls=%async_computation.8 | async-start | bytes 6635520 | tf_op jit(solution)/shard_map/reduce_scatter | solution.py:239
  703.6 204.7 %reduce-scatter.9.cloned.1.call-start = ((), (), s32[]{:S(2)}) async-start(), calls=%async_computation.7 | async-start | bytes 13271040 | tf_op jit(solution)/shard_map/reduce_scatter | solution.py:239
  715.2 217.2 %all-gather.11.cloned.1.call-start = ((), (), s32[]{:S(2)}) async-start(), calls=%async_computation.4 | async-start | bytes 1769472 | tf_op jit(solution)/shard_map/all_gather | solution.py:291
  752.5 179.9 %all-gather.15.cloned.1.call-start = ((), (), s32[]{:S(2)}) async-start(), calls=%async_computation.10 | async-start | bytes 1474560 | tf_op jit(solution)/shard_map/all_gather | solution.py:244
  753.1 182.4 %all-gather.13.cloned.1.call-start = ((), (), s32[]{:S(2)}) async-start(), calls=%async_computation.9 | async-start | bytes 2949120 | tf_op jit(solution)/shard_map/all_gather | solution.py:244
  753.7 191.7 %all-gather.19.cloned.1.call-start = ((), (), s32[]{:S(2)}) async-start(), calls=%async_computation.12 | async-start | bytes 6635520 | tf_op jit(solution)/shard_map/all_gather | solution.py:244
  800.1 331.3 %all-gather.17.cloned.1.call-start = ((), (), s32[]{:S(2)}) async-start(), calls=%async_computation.11 | async-start | bytes 13271040 | tf_op jit(solution)/shard_map/all_gather | solution.py:244
  (105 other events, 2008.6 us)
Sparse Core Ops, SparseCore 0:
  655.8 27.2 reduce-scatter.6
  697.0 37.3 reduce-scatter.4
  738.0 61.9 reduce-scatter.10
  803.6 104.6 reduce-scatter.8
Sparse Core Ops, SparseCore 1:
  752.6 8.4 all-gather.10
  762.5 31.3 all-gather.14
  795.4 49.2 all-gather.12
  846.2 99.1 all-gather.18
  947.0 184.3 all-gather.16
